TPU v7x, 32 devices: a whole 2x2x4 slice. The times are simulated.
32 devices in a mesh: dom: 8 (over z, y), kb: 4 (over x, core).
Axes of the slice: x: 2, y: 2, z: 4, core: 2. Of those that a mesh axis runs over, the one named last changes fastest.
Arguments:
- features: bfloat16 [64, 4096], P(None, ('dom', 'kb')), may hold values from -6 to 6
- vectors: bfloat16 [3, 64, 4096], P(None, None, ('dom', 'kb')), may hold values from -6 to 6
- positions: float32 [3, 4096], P(None, ('dom', 'kb')), may hold values from 0 to 1, as said below
- neighbours: int32 [16, 4096], P(None, ('dom', 'kb')), may hold values from 0 to 384, as said below
- halo_lists: int32 [2, 4096], P(None, ('dom', 'kb')), may hold values from 0 to 127, as said below
- lattice: int32 [3, 2048], replicated, may hold values from -1024 to 1024, as said below
- kspace_filter: float32 [64, 2048], P(None, 'kb'), may hold values from -6 to 6
- node_weight: bfloat16 [64, 64], replicated, may hold values from -0.75 to 0.75
- node_bias: float32 [64], replicated, may hold values from -4 to 4
- message_weight: bfloat16 [64, 192], replicated, may hold values from -0.75 to 0.75
- radial_weight: bfloat16 [20, 192], replicated, may hold values from -3 to 3
- ewald_weight: bfloat16 [64, 64], replicated, may hold values from -0.75 to 0.75
Outputs:
- new_features: bfloat16 [64, 4096], P(None, ('dom', 'kb'))
- new_vectors: bfloat16 [3, 64, 4096], P(None, None, ('dom', 'kb'))
Inputs may be any that keep to these rules, and one draw needn't show every extreme that they name: `neighbours`: entry j of column a names atom a's neighbour in the numbering of E = 385 columns: own atoms, then the atoms received from the device below, then those from the device above; 384 marks an empty slot. Empty slots come last in a column, and each atom has 8 or more filled slots. `halo_lists`: for each device, 128 different local atom numbers in each row. `positions`: atom a's third coordinate times 8 * 4 lies between a // 128 and the next integer. `lattice`: rows 0 and 1 lie between -16 and 16.
All inputs are finite; a program needn't handle non-finite values.
Results may differ from a plain program's by a relative error of at most 0.01.
Values may be sent and summed in bfloat16 or wider, within the bound.
A program may use at most 64 MiB of HBM per device.

v0:
```python
import functools
import math

import jax
import jax.numpy as jnp
import numpy as np
from jax import lax
from jax.experimental import pallas as pl
from jax.experimental.pallas import tpu as pltpu
from jax.sharding import PartitionSpec as P

side_length = 6.0
slab_depth = 6.0
radial_reach = 6.0
distance_floor = 1.0
MESH = pl.DeviceIdType.MESH
f32 = jnp.float32
bf16 = jnp.bfloat16


def polynomial(function, degree):
    nodes = (np.cos((np.arange(degree + 1) + 0.5) * np.pi / (degree + 1)) + 1.0) / 2.0
    fitted = np.polynomial.polynomial.polyfit(nodes, function(nodes / 16.0), degree)
    return [float(value * 16.0**power) for power, value in enumerate(fitted)]


cos_terms = polynomial(lambda w: np.cos(2 * np.pi * np.sqrt(w)), 4)
sin_terms = polynomial(lambda w: np.sin(2 * np.pi * np.sqrt(w)) / np.sqrt(w), 4)


def evaluate(terms, w):
    value = terms[-1] * w + terms[-2]
    for term in terms[-3::-1]:
        value = value * w + term
    return value


def turn_tables(turns):
    part = turns - jnp.floor(turns + 0.5)
    shifted = 0.25 - jnp.abs(part)
    w = shifted * shifted
    cosine = shifted * evaluate(sin_terms, w)
    sine = evaluate(cos_terms, w)
    sine = jnp.where(part < 0.0, -sine, sine)
    return cosine.astype(bf16), sine.astype(bf16)


def over_first(first_operand, second_operand):
    return lax.dot_general(
        first_operand, second_operand, (((0,), (0,)), ((), ())), preferred_element_type=f32
    )


def three_parts(value):
    high = value.astype(bf16)
    rest = value - high.astype(f32)
    middle = rest.astype(bf16)
    low = (rest - middle.astype(f32)).astype(bf16)
    return high.astype(f32), middle.astype(f32), low.astype(f32)


def kernel(
    sizes,
    feat,
    vec,
    pos,
    nbr,
    halo,
    lat,
    kfilter,
    node_weight,
    node_bias,
    message_weight,
    radial_weight,
    ewald_weight,
    out_all,
    group_feat,
    group_pos,
    side_feat,
    side_vec,
    side_pos,
    side_halo,
    cosines,
    sines,
    totals,
    totals_out,
    totals_in,
    filtered,
    filter_rows,
    message_own,
    message_out,
    message_in_slots,
    source_rows,
    group_sems,
    side_sems,
    totals_sems,
    filtered_sems,
    message_sems,
):
    n_dom, n_kb, low_count, norm_scale = sizes
    high_count = n_dom // low_count
    members = low_count * n_kb
    dom, kb = lax.axis_index("dom"), lax.axis_index("kb")
    high, low = lax.div(dom, low_count), lax.rem(dom, low_count)
    me = low * n_kb + kb
    rank = dom * n_kb + kb
    slab_count = n_dom * n_kb
    channels, own = feat.shape
    slots = nbr.shape[0]
    width = kfilter.shape[1] // low_count
    chunk = width // high_count

    def member(steps):
        number = lax.rem(me + steps + members, members)
        return {
            "dom": high * low_count + lax.div(number, n_kb),
            "kb": lax.rem(number, n_kb),
        }

    def level(steps):
        number = lax.rem(high + steps + high_count, high_count)
        return number, {"dom": number * low_count + low, "kb": kb}

    def slab(steps):
        number = lax.rem(rank + steps + slab_count, slab_count)
        return {"dom": lax.div(number, n_kb), "kb": lax.rem(number, n_kb)}

    def remote(source, target, sems, index, device):
        return pltpu.make_async_remote_copy(
            src_ref=source,
            dst_ref=target,
            send_sem=sems.at[(0,) + index],
            recv_sem=sems.at[(1,) + index],
            device_id=device,
            device_id_type=MESH,
        )

    barrier = pltpu.get_barrier_semaphore()
    greeted = [member(d) for d in range(1, members)]
    greeted += [level(d)[1] for d in range(1, high_count)]
    greeted += [slab(1), slab(-1)]
    for device in greeted:
        pl.semaphore_signal(barrier, inc=1, device_id=device, device_id_type=MESH)

    start = pl.multiple_of(kb * (width * low_count) + low * width, math.gcd(width, 128))
    lattice = lat[:, pl.ds(start, width)].astype(f32)
    lattice_high = jnp.floor(lattice[2:3] * 0.0625) * 16.0
    lattice_low = lattice[2:3] - lattice_high
    lattice_parts = jnp.concatenate(
        [lattice[0:1]] * 3
        + [lattice[1:2]] * 3
        + [lattice_high] * 3
        + [lattice_low] * 3
        + [jnp.zeros((4, width), f32)],
        axis=0,
    ).astype(bf16)

    def position_parts(coords):
        rows = []
        for axis in (0, 1, 2, 2):
            rows += list(three_parts(coords[axis : axis + 1]))
        rows.append(jnp.zeros((4, own), f32))
        return jnp.concatenate(rows, axis=0).astype(bf16)

    def tables(slot, coords):
        turns = over_first(lattice_parts, position_parts(coords))
        cosine, sine = turn_tables(turns)
        cosines[:, slot * own : (slot + 1) * own] = cosine
        sines[:, slot * own : (slot + 1) * own] = sine
        return cosine, sine

    def add_totals(slot, cosine, sine, features):
        projected = over_first(features, ewald_weight[...]).astype(bf16)
        both = jnp.concatenate(
            [
                jnp.dot(cosine, projected, preferred_element_type=f32),
                jnp.dot(sine, projected, preferred_element_type=f32),
            ],
            axis=1,
        )
        if slot == 0:
            totals[...] = both
        else:
            totals[...] += both

    pl.semaphore_wait(barrier, len(greeted))
    group_copies = []
    for d in range(1, members):
        device = member(d)
        group_copies.append(remote(pos, group_pos.at[d], group_sems, (0, d), device))
        group_copies.append(remote(feat, group_feat.at[d], group_sems, (1, d), device))
    for copy in group_copies:
        copy.start()
    side_copies = []
    for side, steps in ((0, 1), (1, -1)):
        device = slab(steps)
        side_copies.append(remote(feat, side_feat.at[side], side_sems, (0, side), device))
        side_copies.append(remote(vec, side_vec.at[side], side_sems, (1, side), device))
        side_copies.append(remote(pos, side_pos.at[side], side_sems, (2, side), device))
        side_copies.append(remote(halo, side_halo.at[side], side_sems, (3, side), device))
    for copy in side_copies:
        copy.start()

    transposed = kfilter[...].T
    filter_rows[...] = jnp.concatenate([transposed, transposed], axis=1) * norm_scale
    cosine, sine = tables(0, pos[...])
    add_totals(0, cosine, sine, feat[...])
    for d in range(1, members):
        group_copies[2 * d - 2].wait_recv()
        cosine, sine = tables(d, group_pos[d])
        group_copies[2 * d - 1].wait_recv()
        add_totals(d, cosine, sine, group_feat[d])
    totals_out[...] = totals[...].astype(bf16)

    totals_copies = []
    for d in range(1, high_count):
        number, device = level(d)
        rows = pl.ds(pl.multiple_of(number * chunk, chunk), chunk)
        totals_copies.append(
            remote(totals_out.at[rows], totals_in.at[d], totals_sems, (d,), device)
        )
    near_first = sorted(range(1, high_count), key=lambda d: min(d, high_count - d))
    for d in near_first:
        totals_copies[d - 1].start()

    for copy in side_copies:
        copy.wait_recv()
    bias = jnp.broadcast_to(node_bias[...], (own, channels)).T
    for index, (one_feat, one_vec) in enumerate(
        ((feat, vec), (side_feat.at[0], side_vec.at[0]), (side_feat.at[1], side_vec.at[1]))
    ):
        columns = slice(index * own, (index + 1) * own)
        value = over_first(node_weight[...], one_feat[...]) + bias
        hidden = (value / (1.0 + jnp.exp(-value))).astype(bf16)
        source_rows[: 3 * channels, columns] = over_first(message_weight[...], hidden).astype(bf16)
        source_rows[3 * channels :, columns] = one_vec[...].reshape(3 * channels, own)

    ids = nbr[...]
    reach = halo.shape[1]

    def picked(row, index):
        return jnp.take_along_axis(
            jnp.broadcast_to(row, (slots, row.shape[1])), index, axis=1, mode="promise_in_bounds"
        )

    below_slot = jnp.clip(ids - own, 0, reach - 1)
    above_slot = jnp.clip(ids - (own + reach), 0, reach - 1)
    own_atom = jnp.clip(ids, 0, own - 1)
    below_atom = picked(side_halo[0, 0:1], below_slot)
    above_atom = picked(side_halo[1, 1:2], above_slot)
    is_own = ids < own
    is_below = ids < own + reach
    used = ids < own + 2 * reach
    atoms = jnp.where(
        is_own,
        ids,
        jnp.where(is_below, below_atom + own, jnp.where(used, above_atom + 2 * own, 3 * own)),
    )
    cartesian = []
    for axis in range(3):
        taken = jnp.where(
            is_own,
            picked(pos[axis : axis + 1], own_atom),
            jnp.where(
                is_below,
                picked(side_pos[0, axis : axis + 1], below_atom),
                picked(side_pos[1, axis : axis + 1], above_atom),
            ),
        )
        taken = jnp.where(used, taken, 0.0)
        offset = taken - pos[axis : axis + 1]
        offset = offset - jnp.floor(offset + 0.5)
        cartesian.append(offset * (side_length if axis < 2 else slab_depth * slab_count))
    distance = jnp.sqrt(
        cartesian[0] * cartesian[0] + cartesian[1] * cartesian[1] + cartesian[2] * cartesian[2]
    )
    limit = jnp.maximum(distance, distance_floor)
    direction = [part / limit for part in cartesian]

    radial_count = radial_weight.shape[0]
    spread = 1.5 * radial_reach / radial_count
    centers = lax.broadcasted_iota(jnp.int32, (radial_count, own), 0).astype(f32) * (
        radial_reach / (radial_count - 1)
    )
    numbers = lax.broadcasted_iota(jnp.int32, (3 * own, own), 0)

    def edges(j, sums):
        row = slice(j, j + 1)
        chosen = jnp.where(numbers == atoms[row], 1.0, 0.0).astype(bf16)
        gathered = jnp.dot(source_rows[...], chosen, preferred_element_type=f32)
        scaled = (distance[row] - centers) * (1.0 / spread)
        radial = jnp.exp(-(scaled * scaled)).astype(bf16)
        terms = gathered[: 3 * channels] * over_first(radial_weight[...], radial)
        first = terms[:channels]
        second = terms[channels : 2 * channels]
        third = terms[2 * channels :]
        new = [sums[0] + first]
        for axis in range(3):
            begin = (3 + axis) * channels
            new.append(
                sums[1 + axis]
                + gathered[begin : begin + channels] * second
                + third * direction[axis][row]
            )
        return new

    sums = [jnp.zeros((channels, own), f32)] * 4
    half = slots // 2
    for j in range(half):
        sums = edges(j, sums)

    own_rows = pl.ds(pl.multiple_of(high * chunk, chunk), chunk)
    total = totals[own_rows, :]
    for d in range(1, high_count):
        totals_copies[d - 1].wait_recv()
        total = total + totals_in[d].astype(f32)
    filter_start = pl.multiple_of(low * width + high * chunk, chunk)
    filtered[own_rows, :] = (filter_rows[pl.ds(filter_start, chunk), :] * total).astype(bf16)
    filtered_copies = []
    for d in range(1, high_count):
        filtered_copies.append(
            remote(
                filtered.at[own_rows], filtered.at[own_rows], filtered_sems, (d,), level(d)[1]
            )
        )
    for d in near_first:
        filtered_copies[d - 1].start()

    for j in range(half, slots):
        sums = edges(j, sums)
    for axis in range(3):
        out_all[1 + axis] = (vec[axis].astype(f32) + sums[1 + axis]).astype(bf16)
    message_own[...] = feat[...].astype(f32) + sums[0]

    for copy in filtered_copies:
        copy.wait_recv()
    spectrum = filtered[...]
    real_rows = spectrum.T[:channels]
    imag_rows = spectrum.T[channels:]

    def message_of(d):
        columns = slice(d * own, (d + 1) * own)
        return jnp.dot(
            real_rows, cosines[:, columns], preferred_element_type=f32
        ) + jnp.dot(imag_rows, sines[:, columns], preferred_element_type=f32)

    message_copies = []
    for d in range(1, members):
        message_out[d] = message_of(d).astype(bf16)
        message_copies.append(
            remote(message_out.at[d], message_in_slots.at[d], message_sems, (d,), member(-d))
        )
        message_copies[-1].start()
    result = message_own[...] + message_of(0)
    for copy in message_copies:
        copy.wait_recv()
    for d in range(1, members):
        result = result + message_in_slots[d].astype(f32)
    out_all[0] = result.astype(bf16)
    for copy in group_copies + side_copies + totals_copies + filtered_copies + message_copies:
        copy.wait_send()


def split_kernel(both, out_feat, out_vec):
    out_feat[...] = both[0]
    out_vec[...] = both[1:]


def shards(
    features,
    vectors,
    positions,
    neighbours,
    halo_lists,
    lattice,
    kspace_filter,
    node_weight,
    node_bias,
    message_weight,
    radial_weight,
    ewald_weight,
):
    n_dom, n_kb = lax.axis_size("dom"), lax.axis_size("kb")
    low_count = 1
    high_count = n_dom // low_count
    members = low_count * n_kb
    channels, own = features.shape
    reach = halo_lists.shape[1]
    width = kspace_filter.shape[1] // low_count
    chunk = width // high_count
    norm_scale = 1.0 / math.sqrt(lattice.shape[1] * own * n_dom * n_kb)
    vmem = pl.BlockSpec(memory_space=pltpu.VMEM)
    dma = pltpu.SemaphoreType.DMA
    both = pl.pallas_call(
        functools.partial(kernel, (n_dom, n_kb, low_count, norm_scale)),
        out_shape=jax.ShapeDtypeStruct((4, channels, own), bf16),
        in_specs=[vmem] * 12,
        out_specs=vmem,
        scratch_shapes=[
            pltpu.VMEM((members, channels, own), bf16),
            pltpu.VMEM((members, 3, own), f32),
            pltpu.VMEM((2, channels, own), bf16),
            pltpu.VMEM((2, 3, channels, own), bf16),
            pltpu.VMEM((2, 3, own), f32),
            pltpu.VMEM((2, 2, reach), jnp.int32),
            pltpu.VMEM((width, members * own), bf16),
            pltpu.VMEM((width, members * own), bf16),
            pltpu.VMEM((width, 2 * channels), f32),
            pltpu.VMEM((width, 2 * channels), bf16),
            pltpu.VMEM((high_count, chunk, 2 * channels), bf16),
            pltpu.VMEM((width, 2 * channels), bf16),
            pltpu.VMEM((kspace_filter.shape[1], 2 * channels), f32),
            pltpu.VMEM((channels, own), f32),
            pltpu.VMEM((members, channels, own), bf16),
            pltpu.VMEM((members, channels, own), bf16),
            pltpu.VMEM((6 * channels, 3 * own), bf16),
            dma((2, 2, members)),
            dma((2, 4, 2)),
            dma((2, high_count)),
            dma((2, high_count)),
            dma((2, members)),
        ],
        compiler_params=pltpu.CompilerParams(collective_id=0, has_side_effects=True),
    )(
        features,
        vectors,
        positions,
        neighbours,
        halo_lists,
        lattice,
        kspace_filter,
        node_weight,
        node_bias[None, :],
        message_weight,
        radial_weight,
        ewald_weight,
    )
    return pl.pallas_call(
        split_kernel,
        out_shape=(
            jax.ShapeDtypeStruct(features.shape, bf16),
            jax.ShapeDtypeStruct(vectors.shape, bf16),
        ),
        in_specs=[vmem],
        out_specs=(vmem, vmem),
    )(both)


def solution(mesh):
    atoms = P(None, ("dom", "kb"))
    placed = (
        atoms,
        P(None, None, ("dom", "kb")),
        atoms,
        atoms,
        atoms,
        P(),
        P(None, "kb"),
        P(),
        P(),
        P(),
        P(),
        P(),
    )
    return jax.shard_map(
        shards,
        mesh=mesh,
        in_specs=placed,
        out_specs=(atoms, P(None, None, ("dom", "kb"))),
        check_vma=False,
    )
```

profile of v0, /device:TPU:0, one launch (start us, length us, event | category | flops | bytes accessed | tf_op | source)
XLA Modules:
  0.0 27.0 jit_solution(17713164736136008491)
XLA Ops:
  0.6 24.8 %shard_map.131.both = bf16[4,64,128]{2,1,0:T(8,128)(2,1)} custom-call(bf16[64,128]{1,0:T(8,128)(2,1)} %feat.1, bf16[3,64,128]{2,1,0:T(8,128)(2,1)} %vec.1, f32[3,128]{1,0:T(4,128)} %pos.1, s32[16,128]{1,0:T(8,128)} %nbr.1, s32[2,128]{1,0:T(2,128)} %halo.1, s32[3,2048]{1,0:T(4,128)} %lat.1, f32[64,512]{1,0:T(8,128)} %kfilter.1, bf16[64,64]{1,0:T(8,128)(2,1)} %node_weight.1, ...), custom_call_target="tpu_custom_call" | custom-call | tf_op jit(solution)/shard_map/pallas_call | solution.py:394
  25.5 1.5 %shard_map.132 = (bf16[64,128]{1,0:T(8,128)(2,1)}, bf16[3,64,128]{2,1,0:T(8,128)(2,1)}) custom-call(bf16[4,64,128]{2,1,0:T(8,128)(2,1)} %shard_map.131.both), custom_call_target="tpu_custom_call" | custom-call | tf_op jit(solution)/shard_map/pallas_call | solution.py:438
where the time goes:
time: 27.1 us; the launch traced here: 27 us
  Pallas kernels  26.3 us (97%)
  between operations  0.64 us (2%)
    pallas_call x1, Pallas kernels, shards(): pl.pallas_call(functools.partial(kernel, (n_dom, n_kb, low_count, norm_sc...  24.8 us
    pallas_call x1, Pallas kernels, shards(): pl.pallas_call(split_kernel, out_shape=(jax.ShapeDtypeStruct(features.sha...  1.47 us

commit v1 on v0

--- a/solution.py
+++ b/solution.py
@@ -361,9 +361,13 @@
         copy.wait_send()
 
 
-def split_kernel(both, out_feat, out_vec):
-    out_feat[...] = both[0]
-    out_vec[...] = both[1:]
+def split_kernel(both, out_feat, out_vec, sems):
+    feat_copy = pltpu.make_async_copy(both.at[0], out_feat, sems.at[0])
+    vec_copy = pltpu.make_async_copy(both.at[pl.ds(1, 3)], out_vec, sems.at[1])
+    feat_copy.start()
+    vec_copy.start()
+    feat_copy.wait()
+    vec_copy.wait()
 
 
 def shards(
@@ -393,7 +397,7 @@
     dma = pltpu.SemaphoreType.DMA
     both = pl.pallas_call(
         functools.partial(kernel, (n_dom, n_kb, low_count, norm_scale)),
-        out_shape=jax.ShapeDtypeStruct((4, channels, own), bf16),
+        out_shape=pltpu.VMEM((4, channels, own), bf16),
         in_specs=[vmem] * 12,
         out_specs=vmem,
         scratch_shapes=[
@@ -442,8 +446,9 @@
             jax.ShapeDtypeStruct(vectors.shape, bf16),
         ),
         in_specs=[vmem],
-        out_specs=(vmem, vmem),
-    )(both)
+        out_specs=(pl.BlockSpec(memory_space=pl.ANY),) * 2,
+        scratch_shapes=[dma((2,))],
+    )(pltpu.with_memory_space_constraint(both, pltpu.VMEM))
 
 
 def solution(mesh):

time: 27.1 us -> 25.7 us (0.948)
  Pallas kernels: 26.3 us -> 24.9 us
    pallas_call x1, Pallas kernels: 1.47 us -> 0.65 us  [shards(): pl.pallas_call(split_kernel, out_shape=(jax.ShapeDtypeStruct(features.sha...]
    pallas_call x1, Pallas kernels: 24.8 us -> 24.2 us  [shards(): pl.pallas_call(functools.partial(kernel, (n_dom, n_kb, low_count, norm_sc...]
where the time goes in v1:
time: 25.7 us; the launch traced here: 25.5 us
  Pallas kernels  24.9 us (97%)
  between operations  0.64 us (2%)
    pallas_call x1, Pallas kernels, shards(): pl.pallas_call(functools.partial(kernel, (n_dom, n_kb, low_count, norm_sc...  24.2 us
    pallas_call x1, Pallas kernels, shards(): pl.pallas_call(split_kernel, out_shape=(jax.ShapeDtypeStruct(features.sha...  0.65 us

profile of v1, /device:TPU:0, one launch (start us, length us, event | category | flops | bytes accessed | tf_op | source)
XLA Modules:
  0.0 25.5 jit_solution(16707855670046251114)
XLA Ops:
  0.6 24.2 %shard_map.131.both = bf16[4,64,128]{2,1,0:T(8,128)(2,1)S(1)} custom-call(bf16[64,128]{1,0:T(8,128)(2,1)} %feat.1, bf16[3,64,128]{2,1,0:T(8,128)(2,1)} %vec.1, f32[3,128]{1,0:T(4,128)} %pos.1, s32[16,128]{1,0:T(8,128)} %nbr.1, s32[2,128]{1,0:T(2,128)} %halo.1, s32[3,2048]{1,0:T(4,128)} %lat.1, f32[64,512]{1,0:T(8,128)} %kfilter.1, ...), custom_call_target="tpu_custom_call" | custom-call | tf_op jit(solution)/shard_map/pallas_call | solution.py:398
  24.9 0.6 %shard_map.132 = (bf16[64,128]{1,0:T(8,128)(2,1)}, bf16[3,64,128]{2,1,0:T(8,128)(2,1)}) custom-call(bf16[4,64,128]{2,1,0:T(8,128)(2,1)S(1)} %shard_map.131.both), custom_call_target="tpu_custom_call" | custom-call | tf_op jit(solution)/shard_map/pallas_call | solution.py:442

commit v2 on v1

v2 whole, which is shorter than its diff:
```python
import functools
import math

import jax
import jax.numpy as jnp
import numpy as np
from jax import lax
from jax.experimental import pallas as pl
from jax.experimental.pallas import tpu as pltpu
from jax.sharding import PartitionSpec as P

side_length = 6.0
slab_depth = 6.0
radial_reach = 6.0
distance_floor = 1.0
MESH = pl.DeviceIdType.MESH
f32 = jnp.float32
bf16 = jnp.bfloat16


def polynomial(function, degree):
    nodes = (np.cos((np.arange(degree + 1) + 0.5) * np.pi / (degree + 1)) + 1.0) / 2.0
    fitted = np.polynomial.polynomial.polyfit(nodes, function(nodes / 4.0), degree)
    return [float(value * 4.0**power) for power, value in enumerate(fitted)]


half_cos = polynomial(lambda w: np.sqrt(2.0) * np.cos(np.pi * np.sqrt(w)), 3)
half_sin = polynomial(lambda w: np.sqrt(2.0) * np.sin(np.pi * np.sqrt(w)) / np.sqrt(w), 3)


def evaluate(terms, w):
    value = terms[-1] * w + terms[-2]
    for term in terms[-3::-1]:
        value = value * w + term
    return value


def turn_tables(turns):
    part = turns - jnp.round(turns)
    w = part * part
    sine = part * evaluate(half_sin, w)
    cosine = evaluate(half_cos, w)
    return (1.0 - sine * sine).astype(bf16), (sine * cosine).astype(bf16)


def over_first(first_operand, second_operand):
    return lax.dot_general(
        first_operand, second_operand, (((0,), (0,)), ((), ())), preferred_element_type=f32
    )


def three_parts(value):
    high = value.astype(bf16)
    rest = value - high.astype(f32)
    middle = rest.astype(bf16)
    low = (rest - middle.astype(f32)).astype(bf16)
    return high.astype(f32), middle.astype(f32), low.astype(f32)


def kernel(
    sizes,
    feat_hbm,
    vec_hbm,
    pos_hbm,
    nbr_hbm,
    halo_hbm,
    lat_hbm,
    kfilter_hbm,
    node_weight_hbm,
    node_bias_hbm,
    message_weight_hbm,
    radial_weight_hbm,
    ewald_weight_hbm,
    out_all,
    feat,
    vec,
    pos,
    nbr,
    lat,
    kfilter,
    node_weight,
    node_bias,
    message_weight,
    radial_weight,
    ewald_weight,
    own_projected,
    group_feat,
    group_pos,
    side_rows,
    side_pos,
    side_halo,
    tables,
    near_totals,
    totals_out,
    totals_in,
    filtered,
    message_out,
    message_in_slots,
    source_rows,
    round_sems,
    local_sems,
    pos_sems,
    feat_sems,
    side_sems,
    stage_sems,
):
    n_dom, n_kb, low_count, norm_scale = sizes
    dom, kb = lax.axis_index("dom"), lax.axis_index("kb")
    rank = dom * n_kb + kb
    slab_count = n_dom * n_kb
    channels, own = feat.shape
    slots = nbr.shape[0]
    width = kfilter.shape[1]
    members = n_dom // low_count
    pair = 2 if n_kb % 2 == 0 else 1
    pairs = n_kb // pair
    high, low = lax.div(dom, low_count), lax.rem(dom, low_count)
    peers = n_kb * low_count
    chunk = width // members

    def slot_between(target, source):
        return 1 + source - jnp.where(source > target, 1, 0)

    def member(number):
        return {"dom": number * low_count + low, "kb": kb}

    def peer(slot, sign=1):
        core, across, side = slot % pair, slot // pair % pairs, slot // n_kb
        place = lax.rem(lax.div(kb, pair) + sign * across + pairs, pairs)
        return {
            "dom": high * low_count + lax.rem(low + side, low_count),
            "kb": place * pair + lax.rem(lax.rem(kb, pair) + core, pair),
        }

    others = list(range(1, peers))

    def slab(steps):
        number = lax.rem(rank + steps + slab_count, slab_count)
        return {"dom": lax.div(number, n_kb), "kb": lax.rem(number, n_kb)}

    def remote(source, target, send_sem, recv_sem, device):
        return pltpu.make_async_remote_copy(
            src_ref=source,
            dst_ref=target,
            send_sem=send_sem,
            recv_sem=recv_sem,
            device_id=device,
            device_id_type=MESH,
        )

    def wait_bytes(ref, sem):
        pltpu.make_async_copy(ref, ref, sem).wait()

    barrier = pltpu.get_barrier_semaphore()
    targets = [
        jnp.where(high == 0, members - 1 - index, index + jnp.where(index >= high, 1, 0))
        for index in range(members - 1)
    ]
    greeted = [peer(slot) for slot in range(peers - 1, 0, -1)]
    beside = [(-1, high > 0), (1, high < members - 1)]
    beside_count = sum(jnp.where(there, 1, 0) for steps, there in beside)

    def tell_beside(sem):
        for steps, there in beside:

            @pl.when(there)
            def _(steps=steps):
                pl.semaphore_signal(
                    sem, inc=1, device_id=member(high + steps), device_id_type=MESH
                )

    tell_beside(barrier)
    for device in greeted:
        pl.semaphore_signal(barrier, inc=1, device_id=device, device_id_type=MESH)
    is_last = rank == slab_count - 1

    @pl.when(rank == 0)
    def _():
        pl.semaphore_signal(barrier, inc=1, device_id=slab(-1), device_id_type=MESH)

    start = pl.multiple_of(kb * (width * low_count) + low * width, math.gcd(width, 128))
    filter_start = pl.multiple_of(low * width, math.gcd(width, 128))
    staged = [
        (feat_hbm, feat),
        (ewald_weight_hbm, ewald_weight),
        (pos_hbm, pos),
        (lat_hbm.at[:, pl.ds(start, width)], lat),
        (kfilter_hbm.at[:, pl.ds(filter_start, width)], kfilter),
        (node_weight_hbm, node_weight),
        (node_bias_hbm, node_bias),
        (message_weight_hbm, message_weight),
        (nbr_hbm, nbr),
        (radial_weight_hbm, radial_weight),
        (vec_hbm, vec),
    ]
    local = [
        pltpu.make_async_copy(source, target, local_sems.at[i])
        for i, (source, target) in enumerate(staged)
    ]
    for copy in local:
        copy.start()

    local[0].wait()
    local[1].wait()
    own_projected[...] = over_first(ewald_weight[...], feat[...]).astype(bf16)
    pl.semaphore_wait(barrier, len(greeted) + beside_count + jnp.where(is_last, 1, 0))
    pos_copies = [
        remote(pos_hbm, group_pos.at[slot], pos_sems.at[0], pos_sems.at[1 + slot // pair], peer(slot))
        for slot in others
    ]
    feat_copies = [
        remote(
            own_projected,
            group_feat.at[slot],
            feat_sems.at[0],
            feat_sems.at[1 + slot // pair],
            peer(slot),
        )
        for slot in others
    ]
    for copy in pos_copies + feat_copies[::-1]:
        copy.start()
    rounds = members - 1
    tell_beside(round_sems.at[0])

    def pass_round(number):
        pl.semaphore_wait(round_sems.at[number], beside_count)
        if number + 1 < rounds:
            tell_beside(round_sems.at[number + 1])

    around = [(0, 1, is_last), (1, -1, rank == 0)]
    inside = [
        (side, steps, lax.div(rank + steps + peers, peers) == high + 1)
        for side, steps in ((0, 1), (1, -1))
    ]
    across = [
        (side, steps, jnp.logical_not(jnp.logical_or(ends, within)))
        for (side, steps, ends), (_, _, within) in zip(around, inside)
    ]

    def send_sides(cases):
        for side, steps, chosen in cases:

            @pl.when(chosen)
            def _(side=side, steps=steps):
                send_side(side, steps)


    def send_side(side, steps):
        device = slab(steps)
        for copy in (
            remote(feat_hbm, side_rows.at[side, 0], side_sems.at[0], side_sems.at[3], device),
            remote(
                vec_hbm,
                side_rows.at[side, pl.ds(1, 3)],
                side_sems.at[0],
                side_sems.at[3],
                device,
            ),
            remote(pos_hbm, side_pos.at[side], side_sems.at[1], side_sems.at[4], device),
            remote(halo_hbm, side_halo.at[side], side_sems.at[2], side_sems.at[5], device),
        ):
            copy.start()

    send_sides(around[:1])
    local[2].wait()
    local[3].wait()
    lattice = lat[...].astype(f32)
    lattice_high = jnp.floor(lattice[2:3] * 0.0625) * 16.0
    lattice_low = lattice[2:3] - lattice_high
    lattice_parts = jnp.concatenate(
        [lattice[0:1]] * 3
        + [lattice[1:2]] * 3
        + [lattice_high] * 3
        + [lattice_low] * 3
        + [jnp.zeros((4, width), f32)],
        axis=0,
    ).astype(bf16)

    def position_parts(coords):
        rows = []
        for axis in (0, 1, 2, 2):
            rows += list(three_parts(coords[axis : axis + 1]))
        rows.append(jnp.zeros((4, coords.shape[1]), f32))
        return jnp.concatenate(rows, axis=0).astype(bf16)

    def make_tables(first, coords):
        turns = over_first(lattice_parts, position_parts(coords))
        cosine, sine = turn_tables(turns)
        columns = slice(first * own, first * own + coords.shape[1])
        for number in range(members):
            rows = slice(number * chunk, (number + 1) * chunk)
            tables[2 * number * chunk : (2 * number + 1) * chunk, columns] = cosine[rows]
            tables[(2 * number + 1) * chunk : 2 * (number + 1) * chunk, columns] = sine[rows]

    def totals_of(first, features):
        return lax.dot_general(
            features,
            tables[:, first * own : first * own + features.shape[1]],
            (((1,), (1,)), ((), ())),
            preferred_element_type=f32,
        )

    make_tables(0, pos[...])
    def batch_features(first, count):
        return jnp.concatenate(
            [own_projected[...] if slot == 0 else group_feat[slot] for slot in range(first, first + count)],
            axis=1,
        )

    def wait_features(first, count):
        for slot in range(first - first % pair, first + count, pair):
            begin = max(slot, 1)
            if slot + pair > begin:
                wait_bytes(
                    group_feat.at[pl.ds(begin, slot + pair - begin)], feat_sems.at[1 + slot // pair]
                )

    for slot in range(1, pair):
        wait_bytes(group_pos.at[slot], pos_sems.at[1])
        make_tables(slot, group_pos[slot])
    wait_features(0, pair)
    near_totals[...] = totals_of(0, batch_features(0, pair))
    pass_round(0)
    send_sides(across)
    for first in range(pair, peers, pair):
        wait_bytes(group_pos.at[pl.ds(first, pair)], pos_sems.at[1 + first // pair])
        make_tables(
            first,
            jnp.concatenate([group_pos[slot] for slot in range(first, first + pair)], axis=1),
        )
    wait_features(pair, peers - pair)
    totals = near_totals[...] + totals_of(pair, batch_features(pair, peers - pair))
    for number in range(members):
        totals_out[number] = totals[:, 2 * number * chunk : 2 * (number + 1) * chunk].astype(bf16)
    for number in range(1, rounds - 1):
        pass_round(number)
    for number in targets:
        remote(
            totals_out.at[number],
            totals_in.at[slot_between(number, high)],
            stage_sems.at[0],
            stage_sems.at[1],
            member(number),
        ).start()
    send_sides(inside)
    if rounds > 1:
        pass_round(rounds - 1)
    send_sides(around[1:])

    local[4].wait()
    own_filter = jnp.zeros((channels, chunk), f32)
    for number in range(members):
        part = kfilter[:, number * chunk : (number + 1) * chunk]
        own_filter = jnp.where(high == number, part, own_filter)
    own_filter = jnp.concatenate([own_filter, own_filter], axis=1) * norm_scale
    for copy in local[5:]:
        copy.wait()
    bias = jnp.broadcast_to(node_bias[...], (own, channels)).T

    def fill_sources(index, one_feat, one_vec):
        columns = slice(index * own, (index + 1) * own)
        value = over_first(node_weight[...], one_feat[...]) + bias
        hidden = (value / (1.0 + jnp.exp(-value))).astype(bf16)
        source_rows[: 3 * channels, columns] = over_first(message_weight[...], hidden).astype(bf16)
        source_rows[3 * channels :, columns] = one_vec[...].reshape(3 * channels, own)

    fill_sources(0, feat, vec)
    wait_bytes(totals_in.at[pl.ds(1, members - 1)], stage_sems.at[1])
    total = totals_out[high].astype(f32)
    for slot in range(1, members):
        total = total + totals_in[slot].astype(f32)
    filtered[high] = (own_filter * total).astype(bf16)
    for number in targets:
        remote(
            filtered.at[high],
            filtered.at[high],
            stage_sems.at[4],
            stage_sems.at[5],
            member(number),
        ).start()

    wait_bytes(side_rows, side_sems.at[3])
    wait_bytes(side_pos, side_sems.at[4])
    wait_bytes(side_halo, side_sems.at[5])
    for side in range(2):
        fill_sources(1 + side, side_rows.at[side, 0], side_rows.at[side, pl.ds(1, 3)])
    ids = nbr[...]
    reach = side_halo.shape[2]

    def picked(row, index):
        return jnp.take_along_axis(
            jnp.broadcast_to(row, (slots, row.shape[1])), index, axis=1, mode="promise_in_bounds"
        )

    below_slot = jnp.clip(ids - own, 0, reach - 1)
    above_slot = jnp.clip(ids - (own + reach), 0, reach - 1)
    own_atom = jnp.clip(ids, 0, own - 1)
    below_atom = picked(side_halo[0, 0:1], below_slot)
    above_atom = picked(side_halo[1, 1:2], above_slot)
    is_own = ids < own
    is_below = ids < own + reach
    used = ids < own + 2 * reach
    atoms = jnp.where(
        is_own,
        ids,
        jnp.where(is_below, below_atom + own, jnp.where(used, above_atom + 2 * own, 3 * own)),
    )
    cartesian = []
    for axis in range(3):
        taken = jnp.where(
            is_own,
            picked(pos[axis : axis + 1], own_atom),
            jnp.where(
                is_below,
                picked(side_pos[0, axis : axis + 1], below_atom),
                picked(side_pos[1, axis : axis + 1], above_atom),
            ),
        )
        taken = jnp.where(used, taken, 0.0)
        offset = taken - pos[axis : axis + 1]
        offset = offset - jnp.floor(offset + 0.5)
        cartesian.append(offset * (side_length if axis < 2 else slab_depth * slab_count))
    distance = jnp.sqrt(
        cartesian[0] * cartesian[0] + cartesian[1] * cartesian[1] + cartesian[2] * cartesian[2]
    )
    limit = jnp.maximum(distance, distance_floor)
    direction = [part / limit for part in cartesian]

    radial_count = radial_weight.shape[0]
    spread = 1.5 * radial_reach / radial_count
    centers = lax.broadcasted_iota(jnp.int32, (radial_count, own), 0).astype(f32) * (
        radial_reach / (radial_count - 1)
    )
    numbers = lax.broadcasted_iota(jnp.int32, (3 * own, own), 0)

    def edges(j, sums):
        row = slice(j, j + 1)
        chosen = jnp.where(numbers == atoms[row], 1.0, 0.0).astype(bf16)
        gathered = jnp.dot(source_rows[...], chosen, preferred_element_type=f32)
        scaled = (distance[row] - centers) * (1.0 / spread)
        radial = jnp.exp(-(scaled * scaled)).astype(bf16)
        terms = gathered[: 3 * channels] * over_first(radial_weight[...], radial)
        first = terms[:channels]
        second = terms[channels : 2 * channels]
        third = terms[2 * channels :]
        new = [sums[0] + first]
        for axis in range(3):
            begin = (3 + axis) * channels
            new.append(
                sums[1 + axis]
                + gathered[begin : begin + channels] * second
                + third * direction[axis][row]
            )
        return new

    wait_bytes(filtered.at[pl.ds(1, members - 1)], stage_sems.at[5])
    spectrum = jnp.concatenate([filtered[number] for number in range(members)], axis=1)
    def messages_of(first, last):
        return jnp.dot(
            spectrum, tables[:, first * own : last * own], preferred_element_type=f32
        )

    def send_message(slot, value):
        message_out[slot] = value.astype(bf16)
        remote(
            message_out.at[slot],
            message_in_slots.at[slot],
            stage_sems.at[2],
            stage_sems.at[3],
            peer(slot, -1),
        ).start()

    group = pair * (2 if peers % (2 * pair) == 0 else 1)
    for first in range(peers - group, -1, -group):
        values = messages_of(first, first + group)
        for slot in range(first + group - 1, first - 1, -1):
            value = values[:, (slot - first) * own : (slot - first + 1) * own]
            if slot > 0:
                send_message(slot, value)
            else:
                result = value
    sums = [jnp.zeros((channels, own), f32)] * 4
    half = slots // 2
    for j in range(half):
        sums = edges(j, sums)

    for j in range(half, slots):
        sums = edges(j, sums)
    for axis in range(3):
        out_all[1 + axis] = (vec[axis].astype(f32) + sums[1 + axis]).astype(bf16)
    result = result + feat[...].astype(f32) + sums[0]

    wait_bytes(message_in_slots.at[pl.ds(1, peers - 1)], stage_sems.at[3])
    for d in range(1, peers):
        result = result + message_in_slots[d].astype(f32)
    out_all[0] = result.astype(bf16)
    wait_bytes(group_pos.at[pl.ds(1, peers - 1)], pos_sems.at[0])
    wait_bytes(group_feat.at[pl.ds(1, peers - 1)], feat_sems.at[0])
    wait_bytes(side_rows, side_sems.at[0])
    wait_bytes(side_pos, side_sems.at[1])
    wait_bytes(side_halo, side_sems.at[2])
    wait_bytes(totals_in.at[pl.ds(1, members - 1)], stage_sems.at[0])
    wait_bytes(filtered.at[pl.ds(1, members - 1)], stage_sems.at[4])
    wait_bytes(message_in_slots.at[pl.ds(1, peers - 1)], stage_sems.at[2])


def split_kernel(both, out_feat, out_vec, sems):
    feat_copy = pltpu.make_async_copy(both.at[0], out_feat, sems.at[0])
    vec_copy = pltpu.make_async_copy(both.at[pl.ds(1, 3)], out_vec, sems.at[1])
    feat_copy.start()
    vec_copy.start()
    feat_copy.wait()
    vec_copy.wait()


def shards(
    features,
    vectors,
    positions,
    neighbours,
    halo_lists,
    lattice,
    kspace_filter,
    node_weight,
    node_bias,
    message_weight,
    radial_weight,
    ewald_weight,
):
    n_dom, n_kb = lax.axis_size("dom"), lax.axis_size("kb")
    channels, own = features.shape
    reach = halo_lists.shape[1]
    width = kspace_filter.shape[1]
    low_count = 2 if n_dom % 2 == 0 else 1
    members, peers = n_dom // low_count, n_kb * low_count
    width = width // low_count
    chunk = width // members
    pair = 2 if n_kb % 2 == 0 else 1
    norm_scale = 1.0 / math.sqrt(lattice.shape[1] * own * n_dom * n_kb)
    vmem = pl.BlockSpec(memory_space=pltpu.VMEM)
    hbm = pl.BlockSpec(memory_space=pltpu.HBM)
    dma = pltpu.SemaphoreType.DMA
    bias_row = node_bias[None, :]

    def like(array):
        return pltpu.VMEM(array.shape, array.dtype)

    both = pl.pallas_call(
        functools.partial(kernel, (n_dom, n_kb, low_count, norm_scale)),
        out_shape=pltpu.VMEM((4, channels, own), bf16),
        in_specs=[hbm] * 12,
        out_specs=vmem,
        scratch_shapes=[
            like(features),
            like(vectors),
            like(positions),
            like(neighbours),
            pltpu.VMEM((3, width), jnp.int32),
            pltpu.VMEM((channels, width), f32),
            like(node_weight),
            like(bias_row),
            like(message_weight),
            like(radial_weight),
            like(ewald_weight),
            like(features),
            pltpu.VMEM((peers, channels, own), bf16),
            pltpu.VMEM((peers, 3, own), f32),
            pltpu.VMEM((2, 4, channels, own), bf16),
            pltpu.VMEM((2, 3, own), f32),
            pltpu.VMEM((2, 2, reach), jnp.int32),
            pltpu.VMEM((2 * width, peers * own), bf16),
            pltpu.VMEM((channels, 2 * width), f32),
            pltpu.VMEM((members, channels, 2 * chunk), bf16),
            pltpu.VMEM((members, channels, 2 * chunk), bf16),
            pltpu.VMEM((members, channels, 2 * chunk), bf16),
            pltpu.VMEM((peers, channels, own), bf16),
            pltpu.VMEM((peers, channels, own), bf16),
            pltpu.VMEM((6 * channels, 3 * own), bf16),
            pltpu.SemaphoreType.REGULAR((members - 1,)),
            dma((11,)),
            dma((1 + peers // pair,)),
            dma((1 + peers // pair,)),
            dma((6,)),
            dma((6,)),
        ],
        compiler_params=pltpu.CompilerParams(collective_id=0, has_side_effects=True),
    )(
        features,
        vectors,
        positions,
        neighbours,
        halo_lists,
        lattice,
        kspace_filter,
        node_weight,
        bias_row,
        message_weight,
        radial_weight,
        ewald_weight,
    )
    return pl.pallas_call(
        split_kernel,
        out_shape=(
            jax.ShapeDtypeStruct(features.shape, bf16),
            jax.ShapeDtypeStruct(vectors.shape, bf16),
        ),
        in_specs=[vmem],
        out_specs=(pl.BlockSpec(memory_space=pl.ANY),) * 2,
        scratch_shapes=[dma((2,))],
    )(pltpu.with_memory_space_constraint(both, pltpu.VMEM))


def solution(mesh):
    atoms = P(None, ("dom", "kb"))
    placed = (
        atoms,
        P(None, None, ("dom", "kb")),
        atoms,
        atoms,
        atoms,
        P(),
        P(None, "kb"),
        P(),
        P(),
        P(),
        P(),
        P(),
    )
    return jax.shard_map(
        shards,
        mesh=mesh,
        in_specs=placed,
        out_specs=(atoms, P(None, None, ("dom", "kb"))),
        check_vma=False,
    )
```

time: 25.7 us -> 21.9 us (0.85)
  Pallas kernels: 24.9 us -> 21 us
    pallas_call x1, Pallas kernels: 24.2 us -> 20.4 us  [shards(): pl.pallas_call(functools.partial(kernel, (n_dom, n_kb, low_count, norm_sc...]
where the time goes in v2:
time: 21.9 us; the launch traced here: 21.6 us
  Pallas kernels  21 us (96%)
  between operations  0.64 us (3%)
    pallas_call x1, Pallas kernels, shards(): pl.pallas_call(functools.partial(kernel, (n_dom, n_kb, low_count, norm_sc...  20.4 us
    pallas_call x1, Pallas kernels, shards(): pl.pallas_call(split_kernel, out_shape=(jax.ShapeDtypeStruct(features.sha...  0.65 us

profile of v2, /device:TPU:0, one launch (start us, length us, event | category | flops | bytes accessed | tf_op | source)
XLA Modules:
  0.0 21.6 jit_solution(5910910189049060815)
XLA Ops:
  0.6 20.4 %shard_map.131.both = bf16[4,64,128]{2,1,0:T(8,128)(2,1)S(1)} custom-call(bf16[64,128]{1,0:T(8,128)(2,1)} %feat_hbm.1, bf16[3,64,128]{2,1,0:T(8,128)(2,1)} %vec_hbm.1, f32[3,128]{1,0:T(4,128)} %pos_hbm.1, s32[16,128]{1,0:T(8,128)} %nbr_hbm.1, s32[2,128]{1,0:T(2,128)} %halo_hbm.1, s32[3,2048]{1,0:T(4,128)} %lat_hbm.1, f32[64,512]{1,0:T(8,128)} %kfilter_hbm.1, ...), custom_call_target="tpu_custom_call" | custom-call | tf_op jit(solution)/shard_map/pallas_call | solution.py:549
  21.0 0.6 %shard_map.132 = (bf16[64,128]{1,0:T(8,128)(2,1)}, bf16[3,64,128]{2,1,0:T(8,128)(2,1)}) custom-call(bf16[4,64,128]{2,1,0:T(8,128)(2,1)S(1)} %shard_map.131.both), custom_call_target="tpu_custom_call" | custom-call | tf_op jit(solution)/shard_map/pallas_call | solution.py:602

commit v3 on v2

--- a/solution.py
+++ b/solution.py
@@ -97,12 +97,16 @@
     message_out,
     message_in_slots,
     source_rows,
+    side_total,
+    sent_total,
+    stage_total,
     round_sems,
     local_sems,
     pos_sems,
     feat_sems,
-    side_sems,
+    side_sem,
     stage_sems,
+    send_sem,
 ):
     n_dom, n_kb, low_count, norm_scale = sizes
     dom, kb = lax.axis_index("dom"), lax.axis_index("kb")
@@ -169,9 +173,9 @@
                     sem, inc=1, device_id=member(high + steps), device_id_type=MESH
                 )
 
-    tell_beside(barrier)
     for device in greeted:
         pl.semaphore_signal(barrier, inc=1, device_id=device, device_id_type=MESH)
+    tell_beside(barrier)
     is_last = rank == slab_count - 1
 
     @pl.when(rank == 0)
@@ -194,31 +198,31 @@
         (vec_hbm, vec),
     ]
     local = [
-        pltpu.make_async_copy(source, target, local_sems.at[i])
+        pltpu.make_async_copy(source, target, local_sems.at[0 if i < 4 else 1])
         for i, (source, target) in enumerate(staged)
     ]
     for copy in local:
         copy.start()
 
-    local[0].wait()
-    local[1].wait()
+    for copy in local[:4]:
+        copy.wait()
     own_projected[...] = over_first(ewald_weight[...], feat[...]).astype(bf16)
     pl.semaphore_wait(barrier, len(greeted) + beside_count + jnp.where(is_last, 1, 0))
     pos_copies = [
-        remote(pos_hbm, group_pos.at[slot], pos_sems.at[0], pos_sems.at[1 + slot // pair], peer(slot))
+        remote(pos, group_pos.at[slot], send_sem.at[0], pos_sems.at[slot // pair], peer(slot))
         for slot in others
     ]
     feat_copies = [
         remote(
             own_projected,
             group_feat.at[slot],
-            feat_sems.at[0],
-            feat_sems.at[1 + slot // pair],
+            send_sem.at[0],
+            feat_sems.at[0 if slot < pair else 1],
             peer(slot),
         )
         for slot in others
     ]
-    for copy in pos_copies + feat_copies[::-1]:
+    for copy in pos_copies[::-1] + feat_copies[::-1]:
         copy.start()
     rounds = members - 1
     tell_beside(round_sems.at[0])
@@ -249,22 +253,20 @@
     def send_side(side, steps):
         device = slab(steps)
         for copy in (
-            remote(feat_hbm, side_rows.at[side, 0], side_sems.at[0], side_sems.at[3], device),
+            remote(feat_hbm, side_rows.at[side, 0], send_sem.at[0], side_sem.at[0], device),
             remote(
                 vec_hbm,
                 side_rows.at[side, pl.ds(1, 3)],
-                side_sems.at[0],
-                side_sems.at[3],
+                send_sem.at[0],
+                side_sem.at[0],
                 device,
             ),
-            remote(pos_hbm, side_pos.at[side], side_sems.at[1], side_sems.at[4], device),
-            remote(halo_hbm, side_halo.at[side], side_sems.at[2], side_sems.at[5], device),
+            remote(pos_hbm, side_pos.at[side], send_sem.at[0], side_sem.at[0], device),
+            remote(halo_hbm, side_halo.at[side], send_sem.at[0], side_sem.at[0], device),
         ):
             copy.start()
 
     send_sides(around[:1])
-    local[2].wait()
-    local[3].wait()
     lattice = lat[...].astype(f32)
     lattice_high = jnp.floor(lattice[2:3] * 0.0625) * 16.0
     lattice_low = lattice[2:3] - lattice_high
@@ -309,22 +311,21 @@
         )
 
     def wait_features(first, count):
-        for slot in range(first - first % pair, first + count, pair):
-            begin = max(slot, 1)
-            if slot + pair > begin:
-                wait_bytes(
-                    group_feat.at[pl.ds(begin, slot + pair - begin)], feat_sems.at[1 + slot // pair]
-                )
+        begin = max(first, 1)
+        wait_bytes(
+            group_feat.at[pl.ds(begin, first + count - begin)], feat_sems.at[0 if first < pair else 1]
+        )
 
     for slot in range(1, pair):
-        wait_bytes(group_pos.at[slot], pos_sems.at[1])
+        wait_bytes(group_pos.at[slot], pos_sems.at[0])
         make_tables(slot, group_pos[slot])
-    wait_features(0, pair)
+    if pair > 1:
+        wait_features(0, pair)
     near_totals[...] = totals_of(0, batch_features(0, pair))
     pass_round(0)
     send_sides(across)
     for first in range(pair, peers, pair):
-        wait_bytes(group_pos.at[pl.ds(first, pair)], pos_sems.at[1 + first // pair])
+        wait_bytes(group_pos.at[pl.ds(first, pair)], pos_sems.at[first // pair])
         make_tables(
             first,
             jnp.concatenate([group_pos[slot] for slot in range(first, first + pair)], axis=1),
@@ -335,12 +336,13 @@
         totals_out[number] = totals[:, 2 * number * chunk : 2 * (number + 1) * chunk].astype(bf16)
     for number in range(1, rounds - 1):
         pass_round(number)
-    for number in targets:
+    for index in range(members - 1):
+        number = jnp.where(index < high, high - 1 - index, index + 1)
         remote(
             totals_out.at[number],
             totals_in.at[slot_between(number, high)],
+            send_sem.at[1],
             stage_sems.at[0],
-            stage_sems.at[1],
             member(number),
         ).start()
     send_sides(inside)
@@ -348,14 +350,13 @@
         pass_round(rounds - 1)
     send_sides(around[1:])
 
-    local[4].wait()
+    for copy in local[4:]:
+        copy.wait()
     own_filter = jnp.zeros((channels, chunk), f32)
     for number in range(members):
         part = kfilter[:, number * chunk : (number + 1) * chunk]
         own_filter = jnp.where(high == number, part, own_filter)
     own_filter = jnp.concatenate([own_filter, own_filter], axis=1) * norm_scale
-    for copy in local[5:]:
-        copy.wait()
     bias = jnp.broadcast_to(node_bias[...], (own, channels)).T
 
     def fill_sources(index, one_feat, one_vec):
@@ -366,7 +367,7 @@
         source_rows[3 * channels :, columns] = one_vec[...].reshape(3 * channels, own)
 
     fill_sources(0, feat, vec)
-    wait_bytes(totals_in.at[pl.ds(1, members - 1)], stage_sems.at[1])
+    wait_bytes(totals_in.at[pl.ds(1, members - 1)], stage_sems.at[0])
     total = totals_out[high].astype(f32)
     for slot in range(1, members):
         total = total + totals_in[slot].astype(f32)
@@ -375,14 +376,12 @@
         remote(
             filtered.at[high],
             filtered.at[high],
-            stage_sems.at[4],
-            stage_sems.at[5],
+            send_sem.at[1],
+            stage_sems.at[1],
             member(number),
         ).start()
 
-    wait_bytes(side_rows, side_sems.at[3])
-    wait_bytes(side_pos, side_sems.at[4])
-    wait_bytes(side_halo, side_sems.at[5])
+    wait_bytes(side_total, side_sem.at[0])
     for side in range(2):
         fill_sources(1 + side, side_rows.at[side, 0], side_rows.at[side, pl.ds(1, 3)])
     ids = nbr[...]
@@ -454,7 +453,7 @@
             )
         return new
 
-    wait_bytes(filtered.at[pl.ds(1, members - 1)], stage_sems.at[5])
+    wait_bytes(filtered.at[pl.ds(1, members - 1)], stage_sems.at[1])
     spectrum = jnp.concatenate([filtered[number] for number in range(members)], axis=1)
     def messages_of(first, last):
         return jnp.dot(
@@ -466,8 +465,8 @@
         remote(
             message_out.at[slot],
             message_in_slots.at[slot],
+            send_sem.at[0],
             stage_sems.at[2],
-            stage_sems.at[3],
             peer(slot, -1),
         ).start()
 
@@ -491,23 +490,17 @@
         out_all[1 + axis] = (vec[axis].astype(f32) + sums[1 + axis]).astype(bf16)
     result = result + feat[...].astype(f32) + sums[0]
 
-    wait_bytes(message_in_slots.at[pl.ds(1, peers - 1)], stage_sems.at[3])
+    wait_bytes(message_in_slots.at[pl.ds(1, peers - 1)], stage_sems.at[2])
     for d in range(1, peers):
         result = result + message_in_slots[d].astype(f32)
     out_all[0] = result.astype(bf16)
-    wait_bytes(group_pos.at[pl.ds(1, peers - 1)], pos_sems.at[0])
-    wait_bytes(group_feat.at[pl.ds(1, peers - 1)], feat_sems.at[0])
-    wait_bytes(side_rows, side_sems.at[0])
-    wait_bytes(side_pos, side_sems.at[1])
-    wait_bytes(side_halo, side_sems.at[2])
-    wait_bytes(totals_in.at[pl.ds(1, members - 1)], stage_sems.at[0])
-    wait_bytes(filtered.at[pl.ds(1, members - 1)], stage_sems.at[4])
-    wait_bytes(message_in_slots.at[pl.ds(1, peers - 1)], stage_sems.at[2])
+    wait_bytes(sent_total, send_sem.at[0])
+    wait_bytes(stage_total, send_sem.at[1])
 
 
 def split_kernel(both, out_feat, out_vec, sems):
     feat_copy = pltpu.make_async_copy(both.at[0], out_feat, sems.at[0])
-    vec_copy = pltpu.make_async_copy(both.at[pl.ds(1, 3)], out_vec, sems.at[1])
+    vec_copy = pltpu.make_async_copy(both.at[pl.ds(1, 3)], out_vec, sems.at[0])
     feat_copy.start()
     vec_copy.start()
     feat_copy.wait()
@@ -538,6 +531,10 @@
     chunk = width // members
     pair = 2 if n_kb % 2 == 0 else 1
     norm_scale = 1.0 / math.sqrt(lattice.shape[1] * own * n_dom * n_kb)
+    row_bytes = 128 * 4
+    block_bytes = channels * own * 2
+    side_bytes = 2 * (4 * block_bytes + 3 * own * 4 + 2 * reach * 4)
+    sent_bytes = side_bytes + (peers - 1) * (3 * own * 4 + 2 * block_bytes)
     vmem = pl.BlockSpec(memory_space=pltpu.VMEM)
     hbm = pl.BlockSpec(memory_space=pltpu.HBM)
     dma = pltpu.SemaphoreType.DMA
@@ -577,12 +574,16 @@
             pltpu.VMEM((peers, channels, own), bf16),
             pltpu.VMEM((peers, channels, own), bf16),
             pltpu.VMEM((6 * channels, 3 * own), bf16),
+            pltpu.VMEM((side_bytes // row_bytes, 1, 128), f32),
+            pltpu.VMEM((sent_bytes // row_bytes, 1, 128), f32),
+            pltpu.VMEM((2 * (members - 1), channels, 2 * chunk), bf16),
             pltpu.SemaphoreType.REGULAR((members - 1,)),
-            dma((11,)),
-            dma((1 + peers // pair,)),
-            dma((1 + peers // pair,)),
-            dma((6,)),
-            dma((6,)),
+            dma((2,)),
+            dma((peers // pair,)),
+            dma((2,)),
+            dma((1,)),
+            dma((3,)),
+            dma((2,)),
         ],
         compiler_params=pltpu.CompilerParams(collective_id=0, has_side_effects=True),
     )(
@@ -607,7 +608,7 @@
         ),
         in_specs=[vmem],
         out_specs=(pl.BlockSpec(memory_space=pl.ANY),) * 2,
-        scratch_shapes=[dma((2,))],
+        scratch_shapes=[dma((1,))],
     )(pltpu.with_memory_space_constraint(both, pltpu.VMEM))
 
 

time: 21.9 us -> 21.2 us (0.968)
  Pallas kernels: 21 us -> 20.3 us
    pallas_call x1, Pallas kernels: 20.4 us -> 19.7 us  [shards(): pl.pallas_call(functools.partial(kernel, (n_dom, n_kb, low_count, norm_sc...]
where the time goes in v3:
time: 21.2 us; the launch traced here: 21 us
  Pallas kernels  20.3 us (96%)
  between operations  0.64 us (3%)
    pallas_call x1, Pallas kernels, shards(): pl.pallas_call(functools.partial(kernel, (n_dom, n_kb, low_count, norm_sc...  19.7 us
    pallas_call x1, Pallas kernels, shards(): pl.pallas_call(split_kernel, out_shape=(jax.ShapeDtypeStruct(features.sha...  0.64 us

profile of v3, /device:TPU:0, one launch (start us, length us, event | category | flops | bytes accessed | tf_op | source)
XLA Modules:
  0.0 21.0 jit_solution(447383157928501099)
XLA Ops:
  0.6 19.7 %shard_map.131.both = bf16[4,64,128]{2,1,0:T(8,128)(2,1)S(1)} custom-call(bf16[64,128]{1,0:T(8,128)(2,1)} %feat_hbm.1, bf16[3,64,128]{2,1,0:T(8,128)(2,1)} %vec_hbm.1, f32[3,128]{1,0:T(4,128)} %pos_hbm.1, s32[16,128]{1,0:T(8,128)} %nbr_hbm.1, s32[2,128]{1,0:T(2,128)} %halo_hbm.1, s32[3,2048]{1,0:T(4,128)} %lat_hbm.1, f32[64,512]{1,0:T(8,128)} %kfilter_hbm.1, ...), custom_call_target="tpu_custom_call" | custom-call | tf_op jit(solution)/shard_map/pallas_call | solution.py:546
  20.3 0.6 %shard_map.132 = (bf16[64,128]{1,0:T(8,128)(2,1)}, bf16[3,64,128]{2,1,0:T(8,128)(2,1)}) custom-call(bf16[4,64,128]{2,1,0:T(8,128)(2,1)S(1)} %shard_map.131.both), custom_call_target="tpu_custom_call" | custom-call | tf_op jit(solution)/shard_map/pallas_call | solution.py:603

commit v4 on v3

--- a/solution.py
+++ b/solution.py
@@ -93,6 +93,8 @@
     near_totals,
     totals_out,
     totals_in,
+    totals_all,
+    chunk_filters,
     filtered,
     message_out,
     message_in_slots,
@@ -345,6 +347,17 @@
             stage_sems.at[0],
             member(number),
         ).start()
+
+    @pl.when(high > 0)
+    def _():
+        remote(
+            totals_out.at[pl.ds(1, members - 1)],
+            totals_all.at[high - 1],
+            send_sem.at[1],
+            stage_sems.at[3],
+            member(0),
+        ).start()
+
     send_sides(inside)
     if rounds > 1:
         pass_round(rounds - 1)
@@ -352,11 +365,9 @@
 
     for copy in local[4:]:
         copy.wait()
-    own_filter = jnp.zeros((channels, chunk), f32)
     for number in range(members):
-        part = kfilter[:, number * chunk : (number + 1) * chunk]
-        own_filter = jnp.where(high == number, part, own_filter)
-    own_filter = jnp.concatenate([own_filter, own_filter], axis=1) * norm_scale
+        part = kfilter[:, number * chunk : (number + 1) * chunk] * norm_scale
+        chunk_filters[number] = jnp.concatenate([part, part], axis=1)
     bias = jnp.broadcast_to(node_bias[...], (own, channels)).T
 
     def fill_sources(index, one_feat, one_vec):
@@ -367,12 +378,7 @@
         source_rows[3 * channels :, columns] = one_vec[...].reshape(3 * channels, own)
 
     fill_sources(0, feat, vec)
-    wait_bytes(totals_in.at[pl.ds(1, members - 1)], stage_sems.at[0])
-    total = totals_out[high].astype(f32)
-    for slot in range(1, members):
-        total = total + totals_in[slot].astype(f32)
-    filtered[high] = (own_filter * total).astype(bf16)
-    for number in targets:
+    def send_filtered(number):
         remote(
             filtered.at[high],
             filtered.at[high],
@@ -381,6 +387,60 @@
             member(number),
         ).start()
 
+    wait_bytes(totals_in.at[pl.ds(1, members - 1)], stage_sems.at[0])
+    total = totals_out[high].astype(f32)
+    for slot in range(1, members):
+        total = total + totals_in[slot].astype(f32)
+    filtered[high] = (chunk_filters[high] * total).astype(bf16)
+
+    @pl.when(high > 0)
+    def _():
+        for index in range(members - 2):
+            send_filtered(1 + index + jnp.where(index + 1 >= high, 1, 0))
+
+    @pl.when(high == 0)
+    def _():
+        for number in range(members - 1, 0, -1):
+            send_filtered(number)
+
+    @pl.when(high == 0)
+    def _():
+        wait_bytes(totals_all, stage_sems.at[3])
+        for number in range(1, members):
+            total = totals_out[number].astype(f32)
+            for source in range(members - 1):
+                total = total + totals_all[source, number - 1].astype(f32)
+            filtered[number] = (chunk_filters[number] * total).astype(bf16)
+
+    @pl.when(high > 0)
+    def _():
+        wait_bytes(filtered.at[pl.ds(1, members - 1)], stage_sems.at[1])
+
+    spectrum = jnp.concatenate([filtered[number] for number in range(members)], axis=1)
+    def messages_of(first, last):
+        return jnp.dot(
+            spectrum, tables[:, first * own : last * own], preferred_element_type=f32
+        )
+
+    def send_message(slot, value):
+        message_out[slot] = value.astype(bf16)
+        remote(
+            message_out.at[slot],
+            message_in_slots.at[slot],
+            send_sem.at[0],
+            stage_sems.at[2],
+            peer(slot, -1),
+        ).start()
+
+    group = pair * (2 if peers % (2 * pair) == 0 else 1)
+    for first in range(peers - group, -1, -group):
+        values = messages_of(first, first + group)
+        for slot in range(first + group - 1, first - 1, -1):
+            value = values[:, (slot - first) * own : (slot - first + 1) * own]
+            if slot > 0:
+                send_message(slot, value)
+            else:
+                result = value
     wait_bytes(side_total, side_sem.at[0])
     for side in range(2):
         fill_sources(1 + side, side_rows.at[side, 0], side_rows.at[side, pl.ds(1, 3)])
@@ -453,32 +513,6 @@
             )
         return new
 
-    wait_bytes(filtered.at[pl.ds(1, members - 1)], stage_sems.at[1])
-    spectrum = jnp.concatenate([filtered[number] for number in range(members)], axis=1)
-    def messages_of(first, last):
-        return jnp.dot(
-            spectrum, tables[:, first * own : last * own], preferred_element_type=f32
-        )
-
-    def send_message(slot, value):
-        message_out[slot] = value.astype(bf16)
-        remote(
-            message_out.at[slot],
-            message_in_slots.at[slot],
-            send_sem.at[0],
-            stage_sems.at[2],
-            peer(slot, -1),
-        ).start()
-
-    group = pair * (2 if peers % (2 * pair) == 0 else 1)
-    for first in range(peers - group, -1, -group):
-        values = messages_of(first, first + group)
-        for slot in range(first + group - 1, first - 1, -1):
-            value = values[:, (slot - first) * own : (slot - first + 1) * own]
-            if slot > 0:
-                send_message(slot, value)
-            else:
-                result = value
     sums = [jnp.zeros((channels, own), f32)] * 4
     half = slots // 2
     for j in range(half):
@@ -495,7 +529,13 @@
         result = result + message_in_slots[d].astype(f32)
     out_all[0] = result.astype(bf16)
     wait_bytes(sent_total, send_sem.at[0])
-    wait_bytes(stage_total, send_sem.at[1])
+    @pl.when(high > 0)
+    def _():
+        wait_bytes(stage_total.at[pl.ds(0, 3 * members - 4)], send_sem.at[1])
+
+    @pl.when(high == 0)
+    def _():
+        wait_bytes(stage_total.at[pl.ds(0, 2 * members - 2)], send_sem.at[1])
 
 
 def split_kernel(both, out_feat, out_vec, sems):
@@ -570,19 +610,21 @@
             pltpu.VMEM((channels, 2 * width), f32),
             pltpu.VMEM((members, channels, 2 * chunk), bf16),
             pltpu.VMEM((members, channels, 2 * chunk), bf16),
+            pltpu.VMEM((members - 1, members - 1, channels, 2 * chunk), bf16),
+            pltpu.VMEM((members, channels, 2 * chunk), f32),
             pltpu.VMEM((members, channels, 2 * chunk), bf16),
             pltpu.VMEM((peers, channels, own), bf16),
             pltpu.VMEM((peers, channels, own), bf16),
             pltpu.VMEM((6 * channels, 3 * own), bf16),
             pltpu.VMEM((side_bytes // row_bytes, 1, 128), f32),
             pltpu.VMEM((sent_bytes // row_bytes, 1, 128), f32),
-            pltpu.VMEM((2 * (members - 1), channels, 2 * chunk), bf16),
+            pltpu.VMEM((3 * members, channels, 2 * chunk), bf16),
             pltpu.SemaphoreType.REGULAR((members - 1,)),
             dma((2,)),
             dma((peers // pair,)),
             dma((2,)),
             dma((1,)),
-            dma((3,)),
+            dma((4,)),
             dma((2,)),
         ],
         compiler_params=pltpu.CompilerParams(collective_id=0, has_side_effects=True),

time: 21.2 us -> 20.8 us (0.981)
  the two profiles are of different devices: /device:TPU:0 before, /device:TPU:8 now
where the time goes in v4:
time: 20.8 us; the launch traced here: 20.6 us
  Pallas kernels  20 us (96%)
  between operations  0.64 us (3%)
    pallas_call x1, Pallas kernels, shards(): pl.pallas_call(functools.partial(kernel, (n_dom, n_kb, low_count, norm_sc...  19.3 us
    pallas_call x1, Pallas kernels, shards(): pl.pallas_call(split_kernel, out_shape=(jax.ShapeDtypeStruct(features.sha...  0.64 us

profile of v4, /device:TPU:8, one launch (start us, length us, event | category | flops | bytes accessed | tf_op | source)
XLA Modules:
  0.0 20.6 jit_solution(8068738948956593577)
XLA Ops:
  0.6 19.3 %shard_map.131.both = bf16[4,64,128]{2,1,0:T(8,128)(2,1)S(1)} custom-call(bf16[64,128]{1,0:T(8,128)(2,1)} %feat_hbm.1, bf16[3,64,128]{2,1,0:T(8,128)(2,1)} %vec_hbm.1, f32[3,128]{1,0:T(4,128)} %pos_hbm.1, s32[16,128]{1,0:T(8,128)} %nbr_hbm.1, s32[2,128]{1,0:T(2,128)} %halo_hbm.1, s32[3,2048]{1,0:T(4,128)} %lat_hbm.1, f32[64,512]{1,0:T(8,128)} %kfilter_hbm.1, ...), custom_call_target="tpu_custom_call" | custom-call | tf_op jit(solution)/shard_map/pallas_call | solution.py:586
  20.0 0.6 %shard_map.132 = (bf16[64,128]{1,0:T(8,128)(2,1)}, bf16[3,64,128]{2,1,0:T(8,128)(2,1)}) custom-call(bf16[4,64,128]{2,1,0:T(8,128)(2,1)S(1)} %shard_map.131.both), custom_call_target="tpu_custom_call" | custom-call | tf_op jit(solution)/shard_map/pallas_call | solution.py:645

commit v5 on v4

--- a/solution.py
+++ b/solution.py
@@ -339,7 +339,9 @@
     for number in range(1, rounds - 1):
         pass_round(number)
     for index in range(members - 1):
-        number = jnp.where(index < high, high - 1 - index, index + 1)
+        number = jnp.where(
+            index < high, lax.rem(high - index, jnp.maximum(high, 1)), index + 1
+        )
         remote(
             totals_out.at[number],
             totals_in.at[slot_between(number, high)],

time: 20.8 us -> 20.6 us (level)
  the two profiles are of different devices: /device:TPU:8 before, /device:TPU:0 now
where the time goes in v5:
time: 20.6 us; the launch traced here: 20.4 us
  Pallas kernels  19.7 us (96%)
  between operations  0.64 us (3%)
    pallas_call x1, Pallas kernels, shards(): pl.pallas_call(functools.partial(kernel, (n_dom, n_kb, low_count, norm_sc...  19.1 us
    pallas_call x1, Pallas kernels, shards(): pl.pallas_call(split_kernel, out_shape=(jax.ShapeDtypeStruct(features.sha...  0.64 us

profile of v5, /device:TPU:0, one launch (start us, length us, event | category | flops | bytes accessed | tf_op | source)
XLA Modules:
  0.0 20.4 jit_solution(10496451029038984442)
XLA Ops:
  0.6 19.1 %shard_map.131.both = bf16[4,64,128]{2,1,0:T(8,128)(2,1)S(1)} custom-call(bf16[64,128]{1,0:T(8,128)(2,1)} %feat_hbm.1, bf16[3,64,128]{2,1,0:T(8,128)(2,1)} %vec_hbm.1, f32[3,128]{1,0:T(4,128)} %pos_hbm.1, s32[16,128]{1,0:T(8,128)} %nbr_hbm.1, s32[2,128]{1,0:T(2,128)} %halo_hbm.1, s32[3,2048]{1,0:T(4,128)} %lat_hbm.1, f32[64,512]{1,0:T(8,128)} %kfilter_hbm.1, ...), custom_call_target="tpu_custom_call" | custom-call | tf_op jit(solution)/shard_map/pallas_call | solution.py:588
  19.8 0.6 %shard_map.132 = (bf16[64,128]{1,0:T(8,128)(2,1)}, bf16[3,64,128]{2,1,0:T(8,128)(2,1)}) custom-call(bf16[4,64,128]{2,1,0:T(8,128)(2,1)S(1)} %shard_map.131.both), custom_call_target="tpu_custom_call" | custom-call | tf_op jit(solution)/shard_map/pallas_call | solution.py:647

commit v6 on v4

--- a/solution.py
+++ b/solution.py
@@ -291,7 +291,8 @@
     def make_tables(first, coords):
         turns = over_first(lattice_parts, position_parts(coords))
         cosine, sine = turn_tables(turns)
-        columns = slice(first * own, first * own + coords.shape[1])
+        span = coords.shape[1]
+        columns = pl.ds(pl.multiple_of(first * own, span), span)
         for number in range(members):
             rows = slice(number * chunk, (number + 1) * chunk)
             tables[2 * number * chunk : (2 * number + 1) * chunk, columns] = cosine[rows]
@@ -326,11 +327,23 @@
     near_totals[...] = totals_of(0, batch_features(0, pair))
     pass_round(0)
     send_sides(across)
-    for first in range(pair, peers, pair):
-        wait_bytes(group_pos.at[pl.ds(first, pair)], pos_sems.at[first // pair])
+    order = list(range(1, peers // pair))
+    if pairs == 2 and low_count == 2:
+        place = lax.div(kb, pair)
+        aligned = place == low
+        order = [
+            jnp.where(jnp.logical_and(place == 0, low == 1), 2, 1),
+            jnp.where(aligned, 2, 3),
+            jnp.where(aligned, 3, jnp.where(low == 1, 1, 2)),
+        ]
+    for batch in order:
+        slots_of = [batch * pair + core for core in range(pair)]
+        wait_bytes(
+            group_pos.at[pl.ds(batch * pair, pair)],
+            pos_sems.at[batch],
+        )
         make_tables(
-            first,
-            jnp.concatenate([group_pos[slot] for slot in range(first, first + pair)], axis=1),
+            batch * pair, jnp.concatenate([group_pos[slot] for slot in slots_of], axis=1)
         )
     wait_features(pair, peers - pair)
     totals = near_totals[...] + totals_of(pair, batch_features(pair, peers - pair))
@@ -338,8 +351,7 @@
         totals_out[number] = totals[:, 2 * number * chunk : 2 * (number + 1) * chunk].astype(bf16)
     for number in range(1, rounds - 1):
         pass_round(number)
-    for index in range(members - 1):
-        number = jnp.where(index < high, high - 1 - index, index + 1)
+    def send_totals(number):
         remote(
             totals_out.at[number],
             totals_in.at[slot_between(number, high)],
@@ -348,6 +360,15 @@
             member(number),
         ).start()
 
+    for index in range(members - 1):
+        number = jnp.where(
+            index < high, lax.rem(high - index, jnp.maximum(high, 1)), index + 1
+        )
+
+        @pl.when(jnp.logical_or(number != 1, high <= 1))
+        def _(number=number):
+            send_totals(number)
+
     @pl.when(high > 0)
     def _():
         remote(
@@ -357,6 +378,10 @@
             stage_sems.at[3],
             member(0),
         ).start()
+
+    @pl.when(high > 1)
+    def _():
+        send_totals(1)
 
     send_sides(inside)
     if rounds > 1:

time: 20.8 us -> 20.4 us (0.981)
  the two profiles are of different devices: /device:TPU:8 before, /device:TPU:0 now
where the time goes in v6:
time: 20.4 us; the launch traced here: 20.1 us
  Pallas kernels  19.5 us (96%)
  between operations  0.64 us (3%)
    pallas_call x1, Pallas kernels, shards(): pl.pallas_call(functools.partial(kernel, (n_dom, n_kb, low_count, norm_sc...  18.8 us
    pallas_call x1, Pallas kernels, shards(): pl.pallas_call(split_kernel, out_shape=(jax.ShapeDtypeStruct(features.sha...  0.64 us

profile of v6, /device:TPU:0, one launch (start us, length us, event | category | flops | bytes accessed | tf_op | source)
XLA Modules:
  0.0 20.1 jit_solution(12005475635111074149)
XLA Ops:
  0.6 18.8 %shard_map.131.both = bf16[4,64,128]{2,1,0:T(8,128)(2,1)S(1)} custom-call(bf16[64,128]{1,0:T(8,128)(2,1)} %feat_hbm.1, bf16[3,64,128]{2,1,0:T(8,128)(2,1)} %vec_hbm.1, f32[3,128]{1,0:T(4,128)} %pos_hbm.1, s32[16,128]{1,0:T(8,128)} %nbr_hbm.1, s32[2,128]{1,0:T(2,128)} %halo_hbm.1, s32[3,2048]{1,0:T(4,128)} %lat_hbm.1, f32[64,512]{1,0:T(8,128)} %kfilter_hbm.1, ...), custom_call_target="tpu_custom_call" | custom-call | tf_op jit(solution)/shard_map/pallas_call | solution.py:611
  19.5 0.6 %shard_map.132 = (bf16[64,128]{1,0:T(8,128)(2,1)}, bf16[3,64,128]{2,1,0:T(8,128)(2,1)}) custom-call(bf16[4,64,128]{2,1,0:T(8,128)(2,1)S(1)} %shard_map.131.both), custom_call_target="tpu_custom_call" | custom-call | tf_op jit(solution)/shard_map/pallas_call | solution.py:670

commit v7 on v6

--- a/solution.py
+++ b/solution.py
@@ -365,7 +365,9 @@
             index < high, lax.rem(high - index, jnp.maximum(high, 1)), index + 1
         )
 
-        @pl.when(jnp.logical_or(number != 1, high <= 1))
+        between = jnp.logical_and(number > 0, number < high)
+
+        @pl.when(jnp.logical_not(between))
         def _(number=number):
             send_totals(number)
 
@@ -379,9 +381,12 @@
             member(0),
         ).start()
 
-    @pl.when(high > 1)
-    def _():
-        send_totals(1)
+    for step in range(1, members - 1):
+        number = high - step
+
+        @pl.when(number > 0)
+        def _(number=number):
+            send_totals(number)
 
     send_sides(inside)
     if rounds > 1:

time: 20.4 us -> 20.3 us (level)
    pallas_call x1, Pallas kernels: 18.8 us -> 18.6 us  [shards(): pl.pallas_call(functools.partial(kernel, (n_dom, n_kb, low_count, norm_sc...]
where the time goes in v7:
time: 20.3 us; the launch traced here: 19.9 us
  Pallas kernels  19.3 us (95%)
  between operations  0.64 us (3%)
    pallas_call x1, Pallas kernels, shards(): pl.pallas_call(functools.partial(kernel, (n_dom, n_kb, low_count, norm_sc...  18.6 us
    pallas_call x1, Pallas kernels, shards(): pl.pallas_call(split_kernel, out_shape=(jax.ShapeDtypeStruct(features.sha...  0.64 us

profile of v7, /device:TPU:0, one launch (start us, length us, event | category | flops | bytes accessed | tf_op | source)
XLA Modules:
  0.0 19.9 jit_solution(7718058863935311222)
XLA Ops:
  0.6 18.6 %shard_map.131.both = bf16[4,64,128]{2,1,0:T(8,128)(2,1)S(1)} custom-call(bf16[64,128]{1,0:T(8,128)(2,1)} %feat_hbm.1, bf16[3,64,128]{2,1,0:T(8,128)(2,1)} %vec_hbm.1, f32[3,128]{1,0:T(4,128)} %pos_hbm.1, s32[16,128]{1,0:T(8,128)} %nbr_hbm.1, s32[2,128]{1,0:T(2,128)} %halo_hbm.1, s32[3,2048]{1,0:T(4,128)} %lat_hbm.1, f32[64,512]{1,0:T(8,128)} %kfilter_hbm.1, ...), custom_call_target="tpu_custom_call" | custom-call | tf_op jit(solution)/shard_map/pallas_call | solution.py:616
  19.3 0.6 %shard_map.132 = (bf16[64,128]{1,0:T(8,128)(2,1)}, bf16[3,64,128]{2,1,0:T(8,128)(2,1)}) custom-call(bf16[4,64,128]{2,1,0:T(8,128)(2,1)S(1)} %shard_map.131.both), custom_call_target="tpu_custom_call" | custom-call | tf_op jit(solution)/shard_map/pallas_call | solution.py:675

commit v8 on v7

--- a/solution.py
+++ b/solution.py
@@ -226,7 +226,7 @@
     ]
     for copy in pos_copies[::-1] + feat_copies[::-1]:
         copy.start()
-    rounds = members - 1
+    rounds = members - 2
     tell_beside(round_sems.at[0])
 
     def pass_round(number):
@@ -349,7 +349,7 @@
     totals = near_totals[...] + totals_of(pair, batch_features(pair, peers - pair))
     for number in range(members):
         totals_out[number] = totals[:, 2 * number * chunk : 2 * (number + 1) * chunk].astype(bf16)
-    for number in range(1, rounds - 1):
+    for number in range(1, rounds):
         pass_round(number)
     def send_totals(number):
         remote(
@@ -389,10 +389,6 @@
             send_totals(number)
 
     send_sides(inside)
-    if rounds > 1:
-        pass_round(rounds - 1)
-    send_sides(around[1:])
-
     for copy in local[4:]:
         copy.wait()
     for number in range(members):
@@ -433,6 +429,7 @@
         for number in range(members - 1, 0, -1):
             send_filtered(number)
 
+    send_sides(around[1:])
     @pl.when(high == 0)
     def _():
         wait_bytes(totals_all, stage_sems.at[3])
@@ -649,7 +646,7 @@
             pltpu.VMEM((side_bytes // row_bytes, 1, 128), f32),
             pltpu.VMEM((sent_bytes // row_bytes, 1, 128), f32),
             pltpu.VMEM((3 * members, channels, 2 * chunk), bf16),
-            pltpu.SemaphoreType.REGULAR((members - 1,)),
+            pltpu.SemaphoreType.REGULAR((members - 2,)),
             dma((2,)),
             dma((peers // pair,)),
             dma((2,)),

time: 20.3 us -> 20.3 us (level)
  no operation moved by 1% of the time
where the time goes in v8:
time: 20.3 us; the launch traced here: 19.9 us
  Pallas kernels  19.3 us (95%)
  between operations  0.64 us (3%)
    pallas_call x1, Pallas kernels, shards(): pl.pallas_call(functools.partial(kernel, (n_dom, n_kb, low_count, norm_sc...  18.6 us
    pallas_call x1, Pallas kernels, shards(): pl.pallas_call(split_kernel, out_shape=(jax.ShapeDtypeStruct(features.sha...  0.64 us

profile of v8, /device:TPU:0, one launch (start us, length us, event | category | flops | bytes accessed | tf_op | source)
XLA Modules:
  0.0 19.9 jit_solution(6525310229138895520)
XLA Ops:
  0.6 18.6 %shard_map.131.both = bf16[4,64,128]{2,1,0:T(8,128)(2,1)S(1)} custom-call(bf16[64,128]{1,0:T(8,128)(2,1)} %feat_hbm.1, bf16[3,64,128]{2,1,0:T(8,128)(2,1)} %vec_hbm.1, f32[3,128]{1,0:T(4,128)} %pos_hbm.1, s32[16,128]{1,0:T(8,128)} %nbr_hbm.1, s32[2,128]{1,0:T(2,128)} %halo_hbm.1, s32[3,2048]{1,0:T(4,128)} %lat_hbm.1, f32[64,512]{1,0:T(8,128)} %kfilter_hbm.1, ...), custom_call_target="tpu_custom_call" | custom-call | tf_op jit(solution)/shard_map/pallas_call | solution.py:613
  19.3 0.6 %shard_map.132 = (bf16[64,128]{1,0:T(8,128)(2,1)}, bf16[3,64,128]{2,1,0:T(8,128)(2,1)}) custom-call(bf16[4,64,128]{2,1,0:T(8,128)(2,1)S(1)} %shard_map.131.both), custom_call_target="tpu_custom_call" | custom-call | tf_op jit(solution)/shard_map/pallas_call | solution.py:672

commit v9 on v8

--- a/solution.py
+++ b/solution.py
@@ -200,15 +200,14 @@
         (vec_hbm, vec),
     ]
     local = [
-        pltpu.make_async_copy(source, target, local_sems.at[0 if i < 4 else 1])
+        pltpu.make_async_copy(source, target, local_sems.at[0 if i < 2 else 1 if i < 4 else 2])
         for i, (source, target) in enumerate(staged)
     ]
     for copy in local:
         copy.start()
 
-    for copy in local[:4]:
+    for copy in local[2:4]:
         copy.wait()
-    own_projected[...] = over_first(ewald_weight[...], feat[...]).astype(bf16)
     pl.semaphore_wait(barrier, len(greeted) + beside_count + jnp.where(is_last, 1, 0))
     pos_copies = [
         remote(pos, group_pos.at[slot], send_sem.at[0], pos_sems.at[slot // pair], peer(slot))
@@ -224,7 +223,12 @@
         )
         for slot in others
     ]
-    for copy in pos_copies[::-1] + feat_copies[::-1]:
+    for copy in pos_copies[::-1]:
+        copy.start()
+    for copy in local[:2]:
+        copy.wait()
+    own_projected[...] = over_first(ewald_weight[...], feat[...]).astype(bf16)
+    for copy in feat_copies[::-1]:
         copy.start()
     rounds = members - 2
     tell_beside(round_sems.at[0])
@@ -647,7 +651,7 @@
             pltpu.VMEM((sent_bytes // row_bytes, 1, 128), f32),
             pltpu.VMEM((3 * members, channels, 2 * chunk), bf16),
             pltpu.SemaphoreType.REGULAR((members - 2,)),
-            dma((2,)),
+            dma((3,)),
             dma((peers // pair,)),
             dma((2,)),
             dma((1,)),

time: 20.3 us -> 20.2 us (level); the launches traced: 19.9 us -> 20 us
  no operation moved by 1% of the time
where the time goes in v9:
time: 20.2 us; the launch traced here: 20 us
  Pallas kernels  19.4 us (96%)
  between operations  0.64 us (3%)
    pallas_call x1, Pallas kernels, shards(): pl.pallas_call(functools.partial(kernel, (n_dom, n_kb, low_count, norm_sc...  18.7 us
    pallas_call x1, Pallas kernels, shards(): pl.pallas_call(split_kernel, out_shape=(jax.ShapeDtypeStruct(features.sha...  0.64 us

profile of v9, /device:TPU:0, one launch (start us, length us, event | category | flops | bytes accessed | tf_op | source)
XLA Modules:
  0.0 20.0 jit_solution(2975383014581995038)
XLA Ops:
  0.6 18.7 %shard_map.131.both = bf16[4,64,128]{2,1,0:T(8,128)(2,1)S(1)} custom-call(bf16[64,128]{1,0:T(8,128)(2,1)} %feat_hbm.1, bf16[3,64,128]{2,1,0:T(8,128)(2,1)} %vec_hbm.1, f32[3,128]{1,0:T(4,128)} %pos_hbm.1, s32[16,128]{1,0:T(8,128)} %nbr_hbm.1, s32[2,128]{1,0:T(2,128)} %halo_hbm.1, s32[3,2048]{1,0:T(4,128)} %lat_hbm.1, f32[64,512]{1,0:T(8,128)} %kfilter_hbm.1, ...), custom_call_target="tpu_custom_call" | custom-call | tf_op jit(solution)/shard_map/pallas_call | solution.py:617
  19.4 0.6 %shard_map.132 = (bf16[64,128]{1,0:T(8,128)(2,1)}, bf16[3,64,128]{2,1,0:T(8,128)(2,1)}) custom-call(bf16[4,64,128]{2,1,0:T(8,128)(2,1)S(1)} %shard_map.131.both), custom_call_target="tpu_custom_call" | custom-call | tf_op jit(solution)/shard_map/pallas_call | solution.py:676
